TPU v7x, 256 devices: a whole 4x4x8 slice. The times are simulated.
256 devices in a mesh: chan: 16 (over x, y), kin: 16 (over z, core).
Axes of the slice: x: 4, y: 4, z: 8, core: 2. Of those that a mesh axis runs over, the one named last changes fastest.
Arguments:
- amplitudes: bfloat16 [2048, 512, 512], P(('chan', 'kin')), may hold values from -0.25 to 0.25
- coulomb: bfloat16 [2048, 512, 512], P(('chan', 'kin')), may hold values from -6 to 6
- energies: float32 [2048, 512], P(('chan', 'kin')), may hold values from 0.5 to 3
- orders: int32 [2048], P(('chan', 'kin')), may hold values from 384 to 512, as said below
- partner: int32 [2048], P(('chan', 'kin')), may hold values from 0 to 2047, as said below
- listed: int32 [8192], P(('chan', 'kin')), may hold values from 0 to 122, as said below
- mate_piece: int32 [8192], P(('chan', 'kin')), may hold values from 0 to 511, as said below
Outputs:
- updated: bfloat16 [2048, 512, 512], P(('chan', 'kin'))
Inputs may be any that keep to these rules, and one draw needn't show every extreme that they name: `orders`: each channel's order is one of 384, 448 and 512; a channel and its partner have the same order. partner is an involution without fixed points; the partner of a channel held by the device with chan index i and kin index k is held by the device with chan index i xor (8) and the same kin index. `listed`: the 32 entries of one device are distinct tiles whose tile row and tile column are both below 3. `mate_piece`: the mate relation is an involution without fixed points among the listed pieces of the devices of one chan index; at most 4 pieces of one device have their mates on any one device (itself included), and in every chan index some pair of devices reaches 4.
All inputs are finite; a program needn't handle non-finite values.
Results may differ from a plain program's by a relative error of at most 0.006.
Values may be sent and summed in bfloat16 or wider, within the bound.
No kernel may reach another device: no remote copies, remote signals or barrier semaphores. Data moves between devices by JAX's collectives and lax.ppermute only.
A program may use at most 128 MiB of HBM per device.

v0:
```python
import jax
import jax.numpy as jnp
from jax import lax
from jax.sharding import PartitionSpec as P

CAP = 4


def partner_2(block, axis, stride):
    count = lax.axis_size(axis)
    route = []
    for low in range(count):
        high = low | 1 << stride
        if high != low and high < count:
            route += [(low, high), (high, low)]
    return lax.ppermute(block, axis, route)


def cycle_residual(amp_kept, coul_kept):
    forward = jnp.einsum("cij,cjk->cik", amp_kept, coul_kept, preferred_element_type=jnp.float32)
    forward_half = forward.astype(jnp.bfloat16)
    backward = jnp.einsum("cij,cjk->cik", coul_kept, amp_kept, preferred_element_type=jnp.float32)
    sandwich = jnp.einsum(
        "cij,cjk->cik", forward_half, amp_kept, preferred_element_type=jnp.float32
    )
    return (coul_kept.astype(jnp.float32) + backward + forward + sandwich).astype(jnp.bfloat16)


def tiles_of(blocks):
    local_channels = blocks.shape[0]
    tile_width = blocks.shape[1] // 4
    stacked = blocks.reshape(local_channels, 4, tile_width, 4, tile_width).transpose(0, 1, 3, 2, 4)
    return stacked.reshape(local_channels * 16, tile_width, tile_width)


def on_device(amplitudes, coulomb, energies, orders, partner, listed, mate_piece):
    local_channels = amplitudes.shape[0]
    block_order = amplitudes.shape[1]
    tile_width = block_order // 4
    indices = jnp.arange(block_order, dtype=jnp.int32)
    inside = indices[None, :] < orders[:, None]
    keep_mask = inside[:, :, None] & inside[:, None, :]
    zero_block = jnp.zeros_like(amplitudes)
    amp_kept = jnp.where(keep_mask, amplitudes, zero_block)
    coul_kept = jnp.where(keep_mask, coulomb, zero_block)
    top_bit = lax.axis_size("chan").bit_length() - 2
    pieces = listed.shape[0]
    own_residual = cycle_residual(amp_kept, coul_kept)
    mirrored = partner_2(own_residual, "chan", top_bit)
    partner_slot = partner % local_channels
    mirror_pick = jnp.take(mirrored, partner_slot, axis=0)
    coupled = (
        0.5
        * (own_residual.astype(jnp.float32) + jnp.swapaxes(mirror_pick, 1, 2).astype(jnp.float32))
    ).astype(jnp.bfloat16)
    tile_stack = tiles_of(coupled)
    piece_tiles = jnp.take(tile_stack, listed, axis=0)
    kin_count = lax.axis_size("kin")
    target = mate_piece // pieces
    piece_index = jnp.arange(pieces, dtype=jnp.int32)
    same_target = target[:, None] == target[None, :]
    send_slot = jnp.sum(
        (same_target & (piece_index[None, :] < piece_index[:, None])).astype(jnp.int32), axis=1
    )
    recv_slot = jnp.sum(
        (same_target & (mate_piece[None, :] < mate_piece[:, None])).astype(jnp.int32), axis=1
    )
    buffer_rows = kin_count * CAP
    slot_numbers = jnp.arange(buffer_rows, dtype=jnp.int32)
    routing = (slot_numbers[:, None] == (target * CAP + send_slot)[None, :]).astype(jnp.bfloat16)
    outgoing = jnp.einsum(
        "sp,pij->sij", routing, piece_tiles, preferred_element_type=jnp.float32
    ).astype(jnp.bfloat16)
    incoming = lax.all_to_all(outgoing, "kin", split_axis=0, concat_axis=0, tiled=True)
    mate_tiles = jnp.take(incoming, target * CAP + recv_slot, axis=0)
    exchanged = (
        tile_stack.astype(jnp.float32)
        .at[listed]
        .add(-jnp.swapaxes(mate_tiles, 1, 2).astype(jnp.float32))
    )
    unfolded = exchanged.reshape(local_channels, 4, 4, tile_width, tile_width).transpose(
        0, 1, 3, 2, 4
    )
    unfolded = unfolded.reshape(local_channels, block_order, block_order)
    denominator = energies[:, :, None] + energies[:, None, :]
    return jnp.where(keep_mask, unfolded / denominator, jnp.zeros_like(unfolded)).astype(
        jnp.bfloat16
    )


def solution(mesh):
    return jax.shard_map(
        on_device,
        mesh=mesh,
        in_specs=(
            P(("chan", "kin"), None, None),
            P(("chan", "kin"), None, None),
            P(("chan", "kin"), None),
            P(("chan", "kin")),
            P(("chan", "kin")),
            P(("chan", "kin")),
            P(("chan", "kin")),
        ),
        out_specs=P(("chan", "kin"), None, None),
        check_vma=False,
    )
```

profile of v0, /device:TPU:1, one launch (start us, length us, event | category | flops | bytes accessed | tf_op | source)
XLA Modules:
  0.0 255.3 jit_solution(7214745590484117523)
XLA Ops:
  0.0 0.7 iota_compare_fusion.2
  0.7 7.9 %fusion.7 = f32[8,512,512]{2,1,0:T(8,128)} fusion(bf16[8,512,512]{2,1,0:T(8,128)(2,1)} %param.8, pred[8,512]{1,0:T(8,128)(4,1)S(1)} %iota_compare_fusion.2, bf16[8,512,512]{2,1,0:T(8,128)(2,1)} %param.7), kind=kOutput, calls=%fused_computation.15 | convolution fusion | flops 2155872256 | bytes 16781312 | tf_op jit(solution)/shard_map/cij,cjk->cik/dot_general | solution.py:20
  8.7 5.2 %fusion.8 = f32[8,512,512]{2,1,0:T(8,128)} fusion(bf16[8,512,512]{2,1,0:T(8,128)(2,1)S(1)} %copy-done.2, pred[8,512]{1,0:T(8,128)(4,1)S(1)} %iota_compare_fusion.2, bf16[8,512,512]{2,1,0:T(8,128)(2,1)S(1)} %copy-done.3), kind=kOutput, calls=%fused_computation.16 | convolution fusion | flops 2155872256 | bytes 16781312 | tf_op jit(solution)/shard_map/cij,cjk->cik/dot_general | solution.py:22
  13.9 13.0 %add_convert_fusion = bf16[8,512,512]{2,1,0:T(8,128)(2,1)} fusion(f32[8,512,512]{2,1,0:T(8,128)} %fusion.7, f32[8,512,512]{2,1,0:T(8,128)} %fusion.8, bf16[8,512,512]{2,1,0:T(8,128)(2,1)S(1)} %copy-done.2, pred[8,512]{1,0:T(8,128)(4,1)S(1)} %iota_compare_fusion.2, bf16[8,512,512]{2,1,0:T(8,128)(2,1)} %param.7), kind=kOutput, calls=%fused_computation.12 | convolution fusion | flops 2168455168 | bytes 29364224 | tf_op jit(solution)/shard_map/cij,cjk->cik/dot_general | solution.py:23
  26.9 3.7 %collective-permute-start = (bf16[8,512,512]{2,1,0:T(8,128)(2,1)}, bf16[8,512,512]{2,1,0:T(8,128)(2,1)}, u32[]{:S(2)}, u32[]{:S(2)}) collective-permute-start(bf16[8,512,512]{2,1,0:T(8,128)(2,1)} %add_convert_fusion), channel_id=1, source_target_pairs={{0,128},{128,0},{16,144},{144,16},{32,160},{160,32},{48,176},{176,... | collective-permute-start | bytes 12582920 | tf_op jit(solution)/shard_map/ppermute | solution.py:16
  30.6 6.5 %copy.24 = bf16[8,512,512]{1,2,0:T(8,128)(2,1)} copy(bf16[8,512,512]{2,1,0:T(8,128)(2,1)} %add_convert_fusion) | data formatting | bytes 8388608 | tf_op jit(solution)/shard_map/convert_element_type | solution.py:26
  37.4 82.7 %collective-permute-done = bf16[8,512,512]{2,1,0:T(8,128)(2,1)} collective-permute-done((bf16[8,512,512]{2,1,0:T(8,128)(2,1)}, bf16[8,512,512]{2,1,0:T(8,128)(2,1)}, u32[]{:S(2)}, u32[]{:S(2)}) %collective-permute-start) | collective-permute-done | bytes 4194336 | tf_op jit(solution)/shard_map/ppermute | solution.py:16
  120.2 5.0 %gather_fusion = bf16[8,512,512]{2,1,0:T(8,128)(2,1)} fusion(bf16[8,512,512]{2,1,0:T(8,128)(2,1)} %collective-permute-done, s32[1024]{0:T(1024)S(1)} %pad_clamp_fusion.2), kind=kCustom, calls=%fused_computation | custom fusion | bytes 8388640 | tf_op jit(solution)/shard_map/jit(_take)/gather | solution.py:51
  125.2 7.1 %fusion.2 = bf16[8,512,512]{1,2,0:T(8,128)(2,1)} fusion(bf16[8,512,512]{1,2,0:T(8,128)(2,1)} %copy.24, bf16[8,512,512]{2,1,0:T(8,128)(2,1)} %gather_fusion, pred[8]{0:T(512)(128)(4,1)S(1)} %get-tuple-element.9), kind=kLoop, calls=%fused_computation.10 | loop fusion | flops 12582912 | bytes 12582920 | tf_op jit(solution)/shard_map/convert_element_type | solution.py:55
  132.3 6.9 %reshape.70 = bf16[8,4,128,4,128]{2,1,4,3,0:T(4,128)(2,1)} reshape(bf16[8,512,512]{1,2,0:T(8,128)(2,1)} %fusion.2) | data formatting | bytes 8388608 | tf_op jit(solution)/shard_map/reshape | solution.py:32
  139.2 7.4 %copy.25 = bf16[8,4,4,128,128]{4,3,2,1,0:T(8,128)(2,1)} copy(bf16[8,4,4,128,128]{3,1,4,2,0:T(4,128)(2,1)} %bitcast.23) | data formatting | bytes 8388608 | tf_op jit(solution)/shard_map/transpose | solution.py:32
  146.6 2.9 %gather_fusion.1 = bf16[32,128,128]{2,1,0:T(8,128)(2,1)S(1)} fusion(bf16[128,128,128]{2,1,0:T(8,128)(2,1)} %bitcast.22, s32[1024]{0:T(1024)S(1)} %pad_clamp_fusion.1), kind=kCustom, calls=%fused_computation.1 | custom fusion | bytes 2097280 | tf_op jit(solution)/shard_map/jit(_take)/gather | solution.py:57
  149.7 1.0 convolution_convert_fusion
  150.7 2.7 %copy.27 = bf16[64,128,128]{2,1,0:T(8,128)(2,1)} copy(bf16[64,128,128]{2,0,1:T(8,128)(2,1)S(1)} %convolution_convert_fusion) | data formatting | bytes 4194304 | tf_op jit(solution)/shard_map/convert_element_type | solution.py:73
  153.5 11.0 %all-to-all-start = ((bf16[64,128,128]{2,1,0:T(8,128)(2,1)}), bf16[64,128,128]{2,1,0:T(8,128)(2,1)S(1)}, u32[]{:S(2)}, u32[]{:S(2)}) async-start(bf16[64,128,128]{2,1,0:T(8,128)(2,1)} %copy.27), calls=%async_computation | async-start | bytes 4194304 | tf_op jit(solution)/shard_map/all_to_all | solution.py:74
  164.5 6.5 %bitcast_convert_fusion = f32[128,128,128]{2,1,0:T(8,128)} fusion(bf16[8,4,4,128,128]{4,3,2,1,0:T(8,128)(2,1)} %copy.25), kind=kLoop, calls=%fused_computation.51 | loop fusion | flops 2097152 | bytes 12582912 | tf_op jit(solution)/shard_map/convert_element_type | solution.py:77
  170.9 42.5 %all-to-all-done = bf16[64,128,128]{2,1,0:T(8,128)(2,1)S(1)} async-done(((bf16[64,128,128]{2,1,0:T(8,128)(2,1)}), bf16[64,128,128]{2,1,0:T(8,128)(2,1)S(1)}, u32[]{:S(2)}, u32[]{:S(2)}) %all-to-all-start) | async-done | bytes 2097184 | tf_op jit(solution)/shard_map/all_to_all | solution.py:74
  213.5 0.7 gather_fusion.2
  214.2 1.6 negate_bitcast_fusion
  215.8 1.9 copy.28
  217.8 6.3 %scatter_fusion = f32[128,128,128]{2,1,0:T(8,128)} fusion(f32[128,128,128]{2,1,0:T(8,128)} %bitcast_convert_fusion, s32[32]{0:T(128)S(1)} %compare_select_fusion.1, f32[32,128,128]{2,1,0:T(8,128)S(1)} %copy.28), kind=kCustom, calls=%fused_computation.3 | custom fusion | flops 524288 | bytes 6291584 | tf_op jit(solution)/shard_map/scatter-add | solution.py:79
  224.0 13.8 %copy.33 = f32[8,4,4,128,128]{4,2,3,1,0:T(4,128)} copy(f32[8,4,4,128,128]{4,3,2,1,0:T(8,128)} %bitcast.20) | data formatting | bytes 16777216 | tf_op jit(solution)/shard_map/reshape | solution.py:81
  237.8 10.3 %reshape.73 = f32[8,512,512]{2,1,0:T(8,128)} reshape(f32[8,4,128,4,128]{4,3,2,1,0:T(4,128)} %bitcast.21) | data formatting | bytes 16777216 | tf_op jit(solution)/shard_map/reshape | solution.py:84
  248.1 7.2 %fusion = bf16[8,512,512]{2,1,0:T(8,128)(2,1)} fusion(f32[8,512,512]{2,1,0:T(8,128)} %reshape.73, f32[8,512]{1,0:T(8,128)S(1)} %copy-done, pred[8,512]{1,0:T(8,128)(4,1)S(1)} %iota_compare_fusion.2), kind=kLoop, calls=%fused_computation.7 | loop fusion | flops 10485760 | bytes 12603392 | tf_op jit(solution)/shard_map/convert_element_type | solution.py:86
  (23 shorter events, 0.4 us)
Async XLA Ops:
  0.7 7.9 %copy-start.2 = (bf16[8,512,512]{2,1,0:T(8,128)(2,1)S(1)}, bf16[8,512,512]{2,1,0:T(8,128)(2,1)}, u32[]{:S(2)}) copy-start(bf16[8,512,512]{2,1,0:T(8,128)(2,1)} %param.8) | copy-start | bytes 12582916
  0.7 7.9 %copy-start.3 = (bf16[8,512,512]{2,1,0:T(8,128)(2,1)S(1)}, bf16[8,512,512]{2,1,0:T(8,128)(2,1)}, u32[]{:S(2)}) copy-start(bf16[8,512,512]{2,1,0:T(8,128)(2,1)} %param.7) | copy-start | bytes 12582916
  26.9 10.2 %copy-start.4 = (s32[8]{0:T(128)S(1)}, s32[8]{0:T(128)}, u32[]{:S(2)}) copy-start(s32[8]{0:T(128)} %param.11) | copy-start | bytes 100
  26.9 10.2 %copy-start.5 = (s32[32]{0:T(128)S(1)}, s32[32]{0:T(128)}, u32[]{:S(2)}) copy-start(s32[32]{0:T(128)} %param.12) | copy-start | bytes 388
  26.9 10.3 %copy-start.1 = (s32[32]{0:T(128)S(1)}, s32[32]{0:T(128)}, u32[]{:S(2)}) copy-start(s32[32]{0:T(128)} %param.13) | copy-start | bytes 388
  26.9 93.2 %collective-permute-start = (bf16[8,512,512]{2,1,0:T(8,128)(2,1)}, bf16[8,512,512]{2,1,0:T(8,128)(2,1)}, u32[]{:S(2)}, u32[]{:S(2)}) collective-permute-start(bf16[8,512,512]{2,1,0:T(8,128)(2,1)} %add_convert_fusion), channel_id=1, source_target_pairs={{0,128},{128,0},{16,144},{144,16},{32,160},{160,32},{48,176},{176,... | collective-permute-start | bytes 12582920 | tf_op jit(solution)/shard_map/ppermute | solution.py:16
  153.5 60.0 %all-to-all-start = ((bf16[64,128,128]{2,1,0:T(8,128)(2,1)}), bf16[64,128,128]{2,1,0:T(8,128)(2,1)S(1)}, u32[]{:S(2)}, u32[]{:S(2)}) async-start(bf16[64,128,128]{2,1,0:T(8,128)(2,1)} %copy.27), calls=%async_computation | async-start | bytes 4194304 | tf_op jit(solution)/shard_map/all_to_all | solution.py:74
  237.8 10.3 %copy-start = (f32[8,512]{1,0:T(8,128)S(1)}, f32[8,512]{1,0:T(8,128)}, u32[]{:S(2)}) copy-start(f32[8,512]{1,0:T(8,128)} %param.9) | copy-start | bytes 49156
where the time goes:
time: 256 us; the launch traced here: 255 us
  waiting for transfers between devices  125 us (49%)
  local copies, waits for them, and re-layouts  58.3 us (23%)
  other arithmetic  29.8 us (12%)
  matrix products  27.2 us (11%)
  starting transfers between devices  14.6 us (6%)
    ppermute x1, waiting for transfers between devices, partner_2(): return lax.ppermute(block, axis, route)  82.7 us
    all_to_all x1, waiting for transfers between devices, on_device(): lax.all_to_all(outgoing, 'kin', split_axis=0, concat_axis=0, tiled=True)  42.5 us
    reshape x1, local copies, waits for them, and re-layouts, on_device(): exchanged.reshape(local_channels, 4, 4, tile_width, tile_width)  13.8 us
    dot_general x1, matrix products, cycle_residual(): jnp.einsum('cij,cjk->cik', forward_half, amp_kept, preferred_element_type...  13 us
    all_to_all x1, starting transfers between devices, on_device(): lax.all_to_all(outgoing, 'kin', split_axis=0, concat_axis=0, tiled=True)  11 us
    reshape x1, local copies, waits for them, and re-layouts, on_device(): unfolded = unfolded.reshape(local_channels, block_order, block_order)  10.3 us
    dot_general x1, matrix products, cycle_residual(): jnp.einsum('cij,cjk->cik', amp_kept, coul_kept, preferred_element_type=jn...  7.94 us
    transpose x1, local copies, waits for them, and re-layouts, tiles_of(): blocks.reshape(local_channels, 4, tile_width, 4, tile_width)  7.42 us
  transfers between devices with their start and end apart: 2, of which 2 were waited for; matrix products, arithmetic and copies ran while one was open for 5% of the time, Pallas kernels for 0%

commit v1 on v0

v1 whole, which is shorter than its diff:
```python
import functools

import jax
import jax.numpy as jnp
from jax import lax
from jax.experimental import pallas as pl
from jax.experimental.pallas import tpu as pltpu
from jax.sharding import PartitionSpec as P


CAP = 4
INNER = 3
PER_STEP = 2
BF = jnp.bfloat16
F32 = jnp.float32
ANY = pl.BlockSpec(memory_space=pl.ANY)
WHOLE = pl.BlockSpec(memory_space=pltpu.VMEM)
SMALL = pltpu.CompilerParams(vmem_limit_bytes=6 << 20)


def shell_base(orders, slot, edge, half):
    base = jnp.int32(0)
    for other in range(orders.shape[0]):
        base += jnp.where(other < slot, (orders[other] - edge) // half, 0)
    return base


def residual_channel(orders, amp, coul, lane, slot, own, shell_own):
    block = amp.shape[1]
    tile = block // 4
    half = tile // 2
    edge = INNER * tile
    order = orders[slot]
    rows = lax.broadcasted_iota(jnp.int32, (block, block), 0)
    cols = lax.broadcasted_iota(jnp.int32, (block, block), 1)
    keep = jnp.maximum(rows, cols) < order
    t_kept = jnp.where(keep, amp[lane], jnp.zeros_like(amp[lane]))
    v_kept = jnp.where(keep, coul[lane], jnp.zeros_like(coul[lane]))
    right = v_kept.astype(F32) + jnp.dot(v_kept, t_kept, preferred_element_type=F32)
    both = right + jnp.dot(t_kept, right.astype(BF), preferred_element_type=F32)
    both = both.astype(BF)
    own[slot] = both
    for cut in range(2):
        for col in range(INNER + 1):
            shell_own[slot, cut, col * half : (col + 1) * half] = both[
                edge + cut * half : edge + (cut + 1) * half, col * tile : (col + 1) * tile
            ]
    for row in range(INNER):
        side = both[row * tile : (row + 1) * tile, edge:].T
        for cut in range(2):
            low = (INNER + 1 + row) * half
            shell_own[slot, cut, low : low + half] = side[cut * half : (cut + 1) * half]


def send_channel(orders, slot, own, shell_own, res, shells, res_sem, shell_sem, wait):
    tile = own.shape[1] // 4
    half = tile // 2
    edge = INNER * tile
    whole = pltpu.make_async_copy(own.at[slot], res.at[slot], res_sem.at[slot])
    whole.wait() if wait else whole.start()
    base = jnp.int32(0) if wait else shell_base(orders, slot, edge, half)
    for cut in range(2):
        @pl.when((orders[slot] - edge) // half > cut)
        def _():
            copy = pltpu.make_async_copy(
                shell_own.at[slot, cut], shells.at[base + cut], shell_sem.at[slot, cut]
            )
            copy.wait() if wait else copy.start()


def early_kernel(orders, amp, coul, res, shells, own, shell_own, res_sem, shell_sem):
    step = pl.program_id(0)
    for lane in range(PER_STEP):
        residual_channel(orders, amp, coul, lane, step * PER_STEP + lane, own, shell_own)
    for lane in range(PER_STEP):
        send_channel(orders, step * PER_STEP + lane, own, shell_own, res, shells, res_sem, shell_sem, False)

    @pl.when(step == pl.num_programs(0) - 1)
    def _():
        for slot in range(own.shape[0]):
            send_channel(orders, slot, own, shell_own, res, shells, res_sem, shell_sem, True)


def late_kernel(
    orders, partner, wanted, amp, coul, res_in, shells_in, res, shells, first, second,
    own, shell_own, place, back, res_sem, shell_sem, load_sem, first_sem, second_sem,
):
    del shells_in
    channels = own.shape[0]
    early = channels // 2
    pieces = first.shape[0]
    tile = first.shape[1]
    inner = INNER * INNER
    step = pl.program_id(0)
    load = pltpu.make_async_copy(res_in.at[pl.ds(0, early)], own.at[pl.ds(0, early)], load_sem)

    @pl.when(step == 0)
    def _():
        load.start()
        for slot in range(channels):
            back[partner[slot] % channels] = slot

        def clear(t, carry):
            place[t] = -1
            return carry

        lax.fori_loop(0, channels * inner, clear, 0, unroll=8)

        def mark(p, carry):
            code = wanted[p]
            row = (code % 16) // 4
            col = code % 4
            place[back[code // 16] * inner + col * INNER + row] = p
            return carry

        lax.fori_loop(0, pieces, mark, 0, unroll=4)

        def rank(t, count):
            listed = place[t] >= 0
            place[t] = jnp.where(listed, place[t], pieces + count)
            return count + jnp.where(listed, 0, 1)

        lax.fori_loop(0, channels * inner, rank, 0, unroll=8)

    for lane in range(PER_STEP):
        residual_channel(orders, amp, coul, lane, early + step * PER_STEP + lane, own, shell_own)

    def send_tiles(slot):
        for row in range(INNER):
            for col in range(INNER):
                where = place[slot * inner + row * INNER + col]
                source = own.at[slot, pl.ds(row * tile, tile), pl.ds(col * tile, tile)]

                @pl.when(where < pieces)
                def _():
                    pltpu.make_async_copy(source, first.at[where], first_sem).start()

                @pl.when(where >= pieces)
                def _():
                    pltpu.make_async_copy(source, second.at[where - pieces], second_sem).start()

    for lane in range(PER_STEP):
        send_tiles(early + step * PER_STEP + lane)
    for lane in range(PER_STEP):
        send_channel(
            orders, early + step * PER_STEP + lane, own, shell_own, res, shells, res_sem, shell_sem, False
        )

    @pl.when(step == 0)
    def _():
        load.wait()

        def body(slot, carry):
            send_tiles(slot)
            return carry

        lax.fori_loop(0, early, body, 0)

    @pl.when(step == pl.num_programs(0) - 1)
    def _():
        for slot in range(early, channels):
            send_channel(orders, slot, own, shell_own, res, shells, res_sem, shell_sem, True)
        pltpu.make_async_copy(first, first, first_sem).wait()
        pltpu.make_async_copy(second, second, second_sem).wait()


def residuals(orders, partner, wanted, amp, coul):
    channels, block, _ = amp.shape
    tile = block // 4
    early = channels // 2
    pieces = wanted.shape[0]
    rest = channels * INNER * INNER - pieces
    steps = early // PER_STEP
    res_shape = jax.ShapeDtypeStruct((channels, block, block), BF)
    shell_shape = jax.ShapeDtypeStruct((2 * channels, 7 * tile // 2, tile), BF)
    cost = pl.CostEstimate(
        flops=early * 4 * block**3, bytes_accessed=early * block * block * 8, transcendentals=0
    )

    def scratch(rows):
        return [
            pltpu.VMEM((rows, block, block), BF),
            pltpu.VMEM((rows, 2, 7 * tile // 2, tile), BF),
        ]

    spec = pl.BlockSpec((PER_STEP, block, block), lambda s, *_: (s, 0, 0))
    res, shells = pl.pallas_call(
        early_kernel,
        out_shape=(res_shape, shell_shape),
        grid_spec=pltpu.PrefetchScalarGridSpec(
            num_scalar_prefetch=1,
            grid=(steps,),
            in_specs=[spec, spec],
            out_specs=(ANY, ANY),
            scratch_shapes=scratch(early)
            + [pltpu.SemaphoreType.DMA((early,)), pltpu.SemaphoreType.DMA((early, 2))],
        ),
        cost_estimate=cost,
        name="early",
    )(orders, amp, coul)
    spec = pl.BlockSpec((PER_STEP, block, block), lambda s, *_: (s + steps, 0, 0))
    return pl.pallas_call(
        late_kernel,
        out_shape=(
            res_shape,
            shell_shape,
            jax.ShapeDtypeStruct((pieces, tile, tile), BF),
            jax.ShapeDtypeStruct((rest, tile, tile), BF),
        ),
        grid_spec=pltpu.PrefetchScalarGridSpec(
            num_scalar_prefetch=3,
            grid=(steps,),
            in_specs=[spec, spec, ANY, ANY],
            out_specs=(ANY, ANY, ANY, ANY),
            scratch_shapes=scratch(channels)
            + [
                pltpu.SMEM((channels * INNER * INNER,), jnp.int32),
                pltpu.SMEM((channels,), jnp.int32),
                pltpu.SemaphoreType.DMA((channels,)),
                pltpu.SemaphoreType.DMA((channels, 2)),
                pltpu.SemaphoreType.DMA(()),
                pltpu.SemaphoreType.DMA(()),
                pltpu.SemaphoreType.DMA(()),
            ],
        ),
        input_output_aliases={5: 0, 6: 1},
        cost_estimate=cost,
        name="late",
    )(orders, partner, wanted, amp, coul, res, shells)


def column_of(row, tile):
    return jnp.broadcast_to(row, (tile, tile)).T


def prepare_kernel(listed, energy, res, held, inverse, mine):
    step = pl.program_id(0)
    tile = mine.shape[1]
    across = energy[pl.ds(step, 1), :]
    held[step] = res[0]
    for row in range(INNER + 1):
        down = column_of(across[:, row * tile : (row + 1) * tile], tile)
        for col in range(INNER + 1):
            inverse[step, row * tile : (row + 1) * tile, col * tile : (col + 1) * tile] = 1.0 / (
                down + across[:, col * tile : (col + 1) * tile]
            )

    @pl.when(step == pl.num_programs(0) - 1)
    def _():
        def body(p, carry):
            code = listed[p]
            row = pl.multiple_of((code % 16) // 4 * tile, tile)
            col = pl.multiple_of(code % 4 * tile, tile)
            mine[p] = held[code // 16, pl.ds(row, tile), pl.ds(col, tile)]
            return carry

        lax.fori_loop(0, mine.shape[0], body, 0, unroll=4)


def prepare(listed, energies, res):
    channels, block, _ = res.shape
    tile = block // 4
    return pl.pallas_call(
        prepare_kernel,
        out_shape=(
            jax.ShapeDtypeStruct(res.shape, BF),
            jax.ShapeDtypeStruct(res.shape, F32),
            jax.ShapeDtypeStruct((listed.shape[0], tile, tile), BF),
        ),
        grid_spec=pltpu.PrefetchScalarGridSpec(
            num_scalar_prefetch=1,
            grid=(channels,),
            in_specs=[WHOLE, pl.BlockSpec((1, block, block), lambda s, *_: (s, 0, 0))],
            out_specs=(WHOLE, WHOLE, WHOLE),
        ),
        compiler_params=pltpu.CompilerParams(vmem_limit_bytes=20 << 20),
        name="prepare",
    )(listed, energies, res)


def coupled(own, other):
    return (own + other) * jnp.asarray(0.5, BF)


def couple_kernel(table, mine, theirs, pairs, *outgoing):
    pieces = mine.shape[0]

    def body(p, carry):
        pairs[p] = coupled(mine[p], theirs[p].T)
        return carry

    lax.fori_loop(0, pieces, body, 0, unroll=8)
    for hop, out in enumerate(outgoing):
        for slot in range(CAP):
            out[slot] = pairs[jnp.maximum(table[hop * CAP + slot], 0)]


def couple(table, mine, theirs, peers):
    pieces, tile, _ = mine.shape
    part = jax.ShapeDtypeStruct((CAP, tile, tile), BF)
    return pl.pallas_call(
        couple_kernel,
        out_shape=(jax.ShapeDtypeStruct((pieces, tile, tile), BF),) + (part,) * peers,
        grid_spec=pltpu.PrefetchScalarGridSpec(
            num_scalar_prefetch=1, in_specs=[WHOLE, WHOLE], out_specs=(WHOLE,) * (1 + peers)
        ),
        compiler_params=SMALL,
        name="couple",
    )(table, mine, theirs)


def rest_kernel(orders, spot, base, held, inverse, second, shells, out):
    step = pl.program_id(0)
    tile = second.shape[1]
    half = tile // 2
    inner = INNER * INNER
    edge = INNER * tile
    shell_count = shells.shape[0]
    order = orders[step]

    def put(row, col, other):
        rows = slice(row * tile, (row + 1) * tile)
        cols = slice(col * tile, (col + 1) * tile)
        value = coupled(held[step, rows, cols], other).astype(F32) * inverse[step, rows, cols]
        if max(row, col) == INNER:
            down = lax.broadcasted_iota(jnp.int32, (tile, tile), 0) + row * tile
            across = lax.broadcasted_iota(jnp.int32, (tile, tile), 1) + col * tile
            value = jnp.where(jnp.maximum(down, across) < order, value, 0.0)
        out[0, rows, cols] = value.astype(BF)

    for row in range(INNER):
        for col in range(INNER):
            put(row, col, second[spot[step * inner + row * INNER + col]].T)

    @pl.when(order > edge)
    def _():
        low = jnp.minimum(base[step], shell_count - 1)
        high = jnp.minimum(base[step] + 1, shell_count - 1)

        def joined(unit):
            window = pl.ds(unit * half, half)
            return jnp.concatenate([shells[low, window], shells[high, window]], axis=0)

        for row in range(INNER + 1):
            put(row, INNER, joined(row).T)
        for col in range(INNER):
            put(INNER, col, joined(INNER + 1 + col))

    @pl.when(order <= edge)
    def _():
        out[0, edge:, :] = jnp.zeros((tile, out.shape[2]), BF)
        out[0, :edge, edge:] = jnp.zeros((edge, tile), BF)


def finish_rest(orders, spot, base, held, inverse, second, shells):
    channels, block, _ = held.shape
    return pl.pallas_call(
        rest_kernel,
        out_shape=jax.ShapeDtypeStruct(held.shape, BF),
        grid_spec=pltpu.PrefetchScalarGridSpec(
            num_scalar_prefetch=3,
            grid=(channels,),
            in_specs=[WHOLE, WHOLE, WHOLE, WHOLE],
            out_specs=pl.BlockSpec((1, block, block), lambda s, *_: (s, 0, 0)),
        ),
        compiler_params=SMALL,
        name="rest",
    )(orders, spot, base, held, inverse, second, shells)


def listed_kernel(peers, listed, table, pairs, inverse, *refs):
    incoming, (_, out, mates, made, sem) = refs[:peers], refs[peers:]
    pieces, tile, _ = pairs.shape
    for hop, part in enumerate(incoming):
        for slot in range(CAP):
            piece = table[hop * CAP + slot]
            mates[jnp.where(piece < 0, pieces, piece)] = part[slot]

    def body(p, carry):
        code = listed[p]
        channel = code // 16
        rows = pl.ds(pl.multiple_of((code % 16) // 4 * tile, tile), tile)
        cols = pl.ds(pl.multiple_of(code % 4 * tile, tile), tile)
        value = pairs[p].astype(F32) - mates[p].T.astype(F32)
        made[p] = (value * inverse[channel, rows, cols]).astype(BF)
        pltpu.make_async_copy(made.at[p], out.at[channel, rows, cols], sem).start()
        return carry

    lax.fori_loop(0, pieces, body, 0, unroll=8)
    pltpu.make_async_copy(made, made, sem).wait()


def finish_listed(listed, table, pairs, inverse, incoming, prior):
    pieces, tile, _ = pairs.shape
    peers = len(incoming)
    return pl.pallas_call(
        functools.partial(listed_kernel, peers),
        out_shape=jax.ShapeDtypeStruct(prior.shape, BF),
        grid_spec=pltpu.PrefetchScalarGridSpec(
            num_scalar_prefetch=2,
            in_specs=[WHOLE] * (2 + peers) + [ANY],
            out_specs=ANY,
            scratch_shapes=[
                pltpu.VMEM((pieces + 1, tile, tile), BF),
                pltpu.VMEM((pieces, tile, tile), BF),
                pltpu.SemaphoreType.DMA(()),
            ],
        ),
        input_output_aliases={4 + peers: 0},
        compiler_params=SMALL,
        name="listed",
    )(listed, table, pairs, inverse, *incoming, prior)


def exchange(amplitudes, coulomb, energies, orders, partner, listed, mate_piece):
    channels, block, _ = amplitudes.shape
    tile = block // 4
    pieces = listed.shape[0]
    stride = lax.axis_size("chan") // 2
    peers = lax.axis_size("kin")
    route = [(i, i ^ stride) for i in range(2 * stride)]

    def swap(array):
        return lax.ppermute(array, "chan", route)

    wanted = swap(listed)
    res, shells, first, second = residuals(orders, partner, wanted, amplitudes, coulomb)
    first_in = swap(first)
    second_in = swap(second)
    shells_in = swap(shells)

    listed, partner, mate_piece, orders, energies, res = lax.optimization_barrier(
        (listed, partner, mate_piece, orders, energies, res)
    )
    held, inverse, mine = prepare(listed, energies, res)
    partner_slot = partner % channels
    level = (orders - INNER * tile) // (tile // 2)
    base = jnp.sum(jnp.where(partner_slot[None, :] < partner_slot[:, None], level[None, :], 0), axis=1)
    count = INNER * INNER
    tiles = jnp.arange(channels * count, dtype=jnp.int32)
    slot, row, col = tiles // count, tiles % count // INNER, tiles % INNER
    of_slot = jnp.sum(
        jnp.where(slot[:, None] == jnp.arange(channels, dtype=jnp.int32)[None, :], partner_slot[None, :], 0), axis=1
    )
    key = of_slot * count + col * INNER + row
    unlisted = jnp.all((slot * 16 + row * 4 + col)[:, None] != listed[None, :], axis=1)
    spot = jnp.sum((unlisted[None, :] & (key[None, :] < key[:, None])).astype(jnp.int32), axis=1)
    spot = jnp.minimum(spot, channels * count - pieces - 1)
    me = lax.axis_index("kin")
    target = mate_piece // pieces
    piece_index = jnp.arange(pieces, dtype=jnp.int32)
    same = target[:, None] == target[None, :]
    out_rank = jnp.sum((same & (piece_index[None, :] < piece_index[:, None])).astype(jnp.int32), axis=1)
    in_rank = jnp.sum((same & (mate_piece[None, :] < mate_piece[:, None])).astype(jnp.int32), axis=1)
    places = jnp.arange(peers * CAP, dtype=jnp.int32)

    def table_of(hop, rank):
        hit = places[:, None] == ((hop + peers) % peers * CAP + rank)[None, :]
        return jnp.sum(jnp.where(hit, piece_index[None, :] + 1, 0), axis=1) - 1

    out_table = table_of(target - me, out_rank)
    in_table = table_of(me - target, in_rank)

    pairs, *outgoing = couple(out_table, mine, first_in, peers)
    incoming = [outgoing[0]]
    for hop in range(1, peers):
        incoming.append(
            lax.ppermute(outgoing[hop], "kin", [(k, (k + hop) % peers) for k in range(peers)])
        )
    rest = finish_rest(orders, spot, base, held, inverse, second_in, shells_in)
    return finish_listed(listed, in_table, pairs, inverse, incoming, rest)


def solution(mesh):
    return jax.shard_map(
        exchange,
        mesh=mesh,
        in_specs=(
            P(("chan", "kin"), None, None),
            P(("chan", "kin"), None, None),
            P(("chan", "kin"), None),
            P(("chan", "kin")),
            P(("chan", "kin")),
            P(("chan", "kin")),
            P(("chan", "kin")),
        ),
        out_specs=P(("chan", "kin"), None, None),
        check_vma=False,
    )
```

time: 256 us -> 135 us (0.53)
  waiting for transfers between devices: 125 us -> 67.9 us
  local copies, waits for them, and re-layouts: 58.3 us -> 2.78 us
  other arithmetic: 29.8 us -> 0.91 us
  matrix products: 27.2 us -> 0 us
  Pallas kernels: 0 us -> 24.9 us
  starting transfers between devices: 14.6 us -> 36.1 us
    all_to_all x1 -> x0, waiting for transfers between devices: 42.5 us -> none  [on_device(): lax.all_to_all(outgoing, 'kin', split_axis=0, concat_axis=0, tiled=True)]
    ppermute x1 -> x19, starting transfers between devices: 3.65 us -> 36.1 us  [the longest x15 29.3 us: exchange(): lax.ppermute(outgoing[hop], 'kin', [(k, (k + hop) % peers) for k in range...]
    reshape x3 -> x0, local copies, waits for them, and re-layouts: 31 us -> none  [the longest x1 13.8 us: on_device(): exchanged.reshape(local_channels, 4, 4, tile_width, tile_width)]
    dot_general x4 -> x0, matrix products: 27.2 us -> none  [the longest x1 13 us: cycle_residual(): jnp.einsum('cij,cjk->cik', forward_half, amp_kept, preferred_element_type...]
    pallas_call x0 -> x6, Pallas kernels: none -> 24.9 us  [the longest x1 7.17 us: residuals(): pl.pallas_call(late_kernel, out_shape=(res_shape, shell_shape, jax.ShapeD...]
    convert_element_type x3 -> x0, other arithmetic: 20.8 us -> none  [the longest x1 7.2 us: on_device(): jnp.where(keep_mask, unfolded / denominator, jnp.zeros_like(unfolded))]
    ppermute x1 -> x19, waiting for transfers between devices: 82.7 us -> 67.9 us  [the longest x15 42.2 us: exchange(): lax.ppermute(outgoing[hop], 'kin', [(k, (k + hop) % peers) for k in range...]
    all_to_all x1 -> x0, starting transfers between devices: 11 us -> none  [on_device(): lax.all_to_all(outgoing, 'kin', split_axis=0, concat_axis=0, tiled=True)]
  transfers between devices with their start and end apart: 2 -> 19, of which waited for: 2 -> 11; matrix products, arithmetic and copies ran while one was open for 5% -> 1% of each run, Pallas kernels for 0% -> 12%
where the time goes in v1:
time: 135 us; the launch traced here: 133 us
  waiting for transfers between devices  67.9 us (50%)
  starting transfers between devices  36.1 us (27%)
  Pallas kernels  24.9 us (18%)
  local copies, waits for them, and re-layouts  2.78 us (2%)
    ppermute x15, waiting for transfers between devices, exchange(): lax.ppermute(outgoing[hop], 'kin', [(k, (k + hop) % peers) for k in range...  42.2 us
    ppermute x15, starting transfers between devices, exchange(): lax.ppermute(outgoing[hop], 'kin', [(k, (k + hop) % peers) for k in range...  29.3 us
    ppermute x4, waiting for transfers between devices, swap(): return lax.ppermute(array, 'chan', route)  25.8 us
    pallas_call x1, Pallas kernels, residuals(): pl.pallas_call(late_kernel, out_shape=(res_shape, shell_shape, jax.ShapeD...  7.17 us
    ppermute x4, starting transfers between devices, swap(): return lax.ppermute(array, 'chan', route)  6.78 us
    pallas_call x1, Pallas kernels, residuals(): pl.pallas_call(early_kernel, out_shape=(res_shape, shell_shape), grid_spe...  6.36 us
    pallas_call x1, Pallas kernels, finish_rest(): pl.pallas_call(rest_kernel, out_shape=jax.ShapeDtypeStruct(held.shape, BF...  5.22 us
    pallas_call x1, Pallas kernels, prepare(): pl.pallas_call(prepare_kernel, out_shape=(jax.ShapeDtypeStruct(res.shape,...  2.95 us
  transfers between devices with their start and end apart: 19, of which 11 were waited for; matrix products, arithmetic and copies ran while one was open for 1% of the time, Pallas kernels for 12%

profile of v1, /device:TPU:1, one launch (start us, length us, event | category | flops | bytes accessed | tf_op | source)
XLA Modules:
  0.0 132.9 jit_solution(12139963649872142838)
XLA Ops:
  0.0 3.6 %collective-permute-start = (s32[32]{0:T(128)}, s32[32]{0:T(128)S(1)}, u32[]{:S(2)}, u32[]{:S(2)}) collective-permute-start(s32[32]{0:T(128)} %listed.3), channel_id=1, source_target_pairs={{0,128},{16,144},{32,160},{48,176},{64,192},{80,208},{96,224},{112... | collective-permute-start | bytes 392 | tf_op jit(solution)/shard_map/ppermute | solution.py:424
  3.6 6.4 %early.1 = (bf16[8,512,512]{2,1,0:T(8,128)(2,1)}, bf16[16,448,128]{2,1,0:T(8,128)(2,1)}) custom-call(s32[8]{0:T(128)} %orders.4, bf16[8,512,512]{2,1,0:T(8,128)(2,1)} %amp.3, bf16[8,512,512]{2,1,0:T(8,128)(2,1)} %coul.3), custom_call_target="tpu_custom_call" | custom-call | flops 2147483648 | bytes 8388608 | tf_op jit(solution)/shard_map/early/pallas_call | solution.py:187
  10.5 7.2 %late.1 = (bf16[8,512,512]{2,1,0:T(8,128)(2,1)}, bf16[16,448,128]{2,1,0:T(8,128)(2,1)}, bf16[32,128,128]{2,1,0:T(8,128)(2,1)}, bf16[40,128,128]{2,1,0:T(8,128)(2,1)}) custom-call(s32[8]{0:T(128)} %orders.4, s32[8]{0:T(128)} %partner.1, s32[32]{0:T(128)} %copy-done.6, bf16[8,512,512]{2,1,0:T(8,128)(2,1)} %amp.3, ...), custom_call_target="tpu_custom_call", output_to_operand_aliasing={{0}: (5, {}), {1}: (6, {})} | custom-call | flops 2147483648 | bytes 8388608 | tf_op jit(solution)/shard_map/late/pallas_call | solution.py:202
  17.9 3.0 %collective-permute-start.18 = (bf16[16,448,128]{2,1,0:T(8,128)(2,1)}, bf16[16,448,128]{2,1,0:T(8,128)(2,1)S(1)}, u32[]{:S(2)}, u32[]{:S(2)}) collective-permute-start(bf16[16,448,128]{2,1,0:T(8,128)(2,1)} %get-tuple-element.68), channel_id=1, source_target_pairs={{0,128},{16,144},{32,160},{48,176},{64,192},{80,208},{96,224},{112... | collective-permute-start | bytes 5505032 | tf_op jit(solution)/shard_map/ppermute | solution.py:424
  21.0 2.2 %copy-done = bf16[8,512,512]{2,1,0:T(8,128)(2,1)S(1)} copy-done((bf16[8,512,512]{2,1,0:T(8,128)(2,1)S(1)}, bf16[8,512,512]{2,1,0:T(8,128)(2,1)}, u32[]{:S(2)}) %copy-start) | copy-done | bytes 4194328
  23.2 2.9 %prepare.1 = (bf16[8,512,512]{2,1,0:T(8,128)(2,1)S(1)}, f32[8,512,512]{2,1,0:T(8,128)S(1)}, bf16[32,128,128]{2,1,0:T(8,128)(2,1)S(1)}) custom-call(s32[32]{0:T(128)S(1)} %copy-done.3, f32[8,512]{1,0:T(8,128)S(1)} %copy-done.1, bf16[8,512,512]{2,1,0:T(8,128)(2,1)S(1)} %copy-done), custom_call_target="tpu_custom_call" | custom-call | tf_op jit(solution)/shard_map/prepare/pallas_call | solution.py:263
  26.5 16.7 %collective-permute-done.1.theirs = bf16[32,128,128]{2,1,0:T(8,128)(2,1)S(1)} collective-permute-done((bf16[32,128,128]{2,1,0:T(8,128)(2,1)}, bf16[32,128,128]{2,1,0:T(8,128)(2,1)S(1)}, u32[]{:S(2)}, u32[]{:S(2)}) %collective-permute-start.1) | collective-permute-done | bytes 1048608 | tf_op jit(solution)/shard_map/ppermute | solution.py:424
  43.3 1.2 couple.1
  44.5 9.6 %collective-permute-start.10 = (bf16[4,128,128]{2,1,0:T(8,128)(2,1)S(1)}, bf16[4,128,128]{2,1,0:T(8,128)(2,1)S(1)}, u32[]{:S(2)}, u32[]{:S(2)}) collective-permute-start(bf16[4,128,128]{2,1,0:T(8,128)(2,1)S(1)} %get-tuple-element.57), channel_id=1, source_target_pairs={{0,9},{1,10},{2,11},{3,12},{4,13},{5,14},{6,15},{7,0},{8,1},{9,2},... | collective-permute-start | bytes 393224 | tf_op jit(solution)/shard_map/ppermute | solution.py:468
  54.2 2.0 %collective-permute-start.12 = (bf16[4,128,128]{2,1,0:T(8,128)(2,1)S(1)}, bf16[4,128,128]{2,1,0:T(8,128)(2,1)S(1)}, u32[]{:S(2)}, u32[]{:S(2)}) collective-permute-start(bf16[4,128,128]{2,1,0:T(8,128)(2,1)S(1)} %get-tuple-element.59), channel_id=1, source_target_pairs={{0,11},{1,12},{2,13},{3,14},{4,15},{5,0},{6,1},{7,2},{8,3},{9,4},{... | collective-permute-start | bytes 393224 | tf_op jit(solution)/shard_map/ppermute | solution.py:468
  56.2 8.0 %collective-permute-done.10.refs_9_ = bf16[4,128,128]{2,1,0:T(8,128)(2,1)S(1)} collective-permute-done((bf16[4,128,128]{2,1,0:T(8,128)(2,1)S(1)}, bf16[4,128,128]{2,1,0:T(8,128)(2,1)S(1)}, u32[]{:S(2)}, u32[]{:S(2)}) %collective-permute-start.10) | collective-permute-done | bytes 131104 | tf_op jit(solution)/shard_map/ppermute | solution.py:468
  64.6 8.9 %collective-permute-done.11.refs_10_ = bf16[4,128,128]{2,1,0:T(8,128)(2,1)S(1)} collective-permute-done((bf16[4,128,128]{2,1,0:T(8,128)(2,1)S(1)}, bf16[4,128,128]{2,1,0:T(8,128)(2,1)S(1)}, u32[]{:S(2)}, u32[]{:S(2)}) %collective-permute-start.11) | collective-permute-done | bytes 131104 | tf_op jit(solution)/shard_map/ppermute | solution.py:468
  73.5 6.1 %collective-permute-done.12.refs_11_ = bf16[4,128,128]{2,1,0:T(8,128)(2,1)S(1)} collective-permute-done((bf16[4,128,128]{2,1,0:T(8,128)(2,1)S(1)}, bf16[4,128,128]{2,1,0:T(8,128)(2,1)S(1)}, u32[]{:S(2)}, u32[]{:S(2)}) %collective-permute-start.12) | collective-permute-done | bytes 131104 | tf_op jit(solution)/shard_map/ppermute | solution.py:468
  79.7 3.9 %collective-permute-done.13.refs_12_ = bf16[4,128,128]{2,1,0:T(8,128)(2,1)S(1)} collective-permute-done((bf16[4,128,128]{2,1,0:T(8,128)(2,1)S(1)}, bf16[4,128,128]{2,1,0:T(8,128)(2,1)S(1)}, u32[]{:S(2)}, u32[]{:S(2)}) %collective-permute-start.13) | collective-permute-done | bytes 131104 | tf_op jit(solution)/shard_map/ppermute | solution.py:468
  83.9 2.5 %collective-permute-done.14.refs_13_ = bf16[4,128,128]{2,1,0:T(8,128)(2,1)S(1)} collective-permute-done((bf16[4,128,128]{2,1,0:T(8,128)(2,1)S(1)}, bf16[4,128,128]{2,1,0:T(8,128)(2,1)S(1)}, u32[]{:S(2)}, u32[]{:S(2)}) %collective-permute-start.14) | collective-permute-done | bytes 131104 | tf_op jit(solution)/shard_map/ppermute | solution.py:468
  87.4 1.8 %collective-permute-done.15.refs_14_ = bf16[4,128,128]{2,1,0:T(8,128)(2,1)S(1)} collective-permute-done((bf16[4,128,128]{2,1,0:T(8,128)(2,1)S(1)}, bf16[4,128,128]{2,1,0:T(8,128)(2,1)S(1)}, u32[]{:S(2)}, u32[]{:S(2)}) %collective-permute-start.15) | collective-permute-done | bytes 131104 | tf_op jit(solution)/shard_map/ppermute | solution.py:468
  90.9 2.2 %collective-permute-start.5 = (bf16[4,128,128]{2,1,0:T(8,128)(2,1)S(1)}, bf16[4,128,128]{2,1,0:T(8,128)(2,1)S(1)}, u32[]{:S(2)}, u32[]{:S(2)}) collective-permute-start(bf16[4,128,128]{2,1,0:T(8,128)(2,1)S(1)} %get-tuple-element.52), channel_id=1, source_target_pairs={{0,4},{1,5},{2,6},{3,7},{4,8},{5,9},{6,10},{7,11},{8,12},{9,13},{1... | collective-permute-start | bytes 393224 | tf_op jit(solution)/shard_map/ppermute | solution.py:468
  93.1 3.5 %collective-permute-done.3.refs_2_ = bf16[4,128,128]{2,1,0:T(8,128)(2,1)S(1)} collective-permute-done((bf16[4,128,128]{2,1,0:T(8,128)(2,1)S(1)}, bf16[4,128,128]{2,1,0:T(8,128)(2,1)S(1)}, u32[]{:S(2)}, u32[]{:S(2)}) %collective-permute-start.3) | collective-permute-done | bytes 131104 | tf_op jit(solution)/shard_map/ppermute | solution.py:468
  98.0 3.7 %collective-permute-start.7 = (bf16[4,128,128]{2,1,0:T(8,128)(2,1)S(1)}, bf16[4,128,128]{2,1,0:T(8,128)(2,1)S(1)}, u32[]{:S(2)}, u32[]{:S(2)}) collective-permute-start(bf16[4,128,128]{2,1,0:T(8,128)(2,1)S(1)} %get-tuple-element.54), channel_id=1, source_target_pairs={{0,6},{1,7},{2,8},{3,9},{4,10},{5,11},{6,12},{7,13},{8,14},{9,15},... | collective-permute-start | bytes 393224 | tf_op jit(solution)/shard_map/ppermute | solution.py:468
  101.7 9.0 %collective-permute-done.17.second = bf16[40,128,128]{2,1,0:T(8,128)(2,1)S(1)} collective-permute-done((bf16[40,128,128]{2,1,0:T(8,128)(2,1)}, bf16[40,128,128]{2,1,0:T(8,128)(2,1)S(1)}, u32[]{:S(2)}, u32[]{:S(2)}) %collective-permute-start.17) | collective-permute-done | bytes 1310752 | tf_op jit(solution)/shard_map/ppermute | solution.py:424
  110.7 8.5 %collective-permute-start.8 = (bf16[4,128,128]{2,1,0:T(8,128)(2,1)S(1)}, bf16[4,128,128]{2,1,0:T(8,128)(2,1)S(1)}, u32[]{:S(2)}, u32[]{:S(2)}) collective-permute-start(bf16[4,128,128]{2,1,0:T(8,128)(2,1)S(1)} %get-tuple-element.55), channel_id=1, source_target_pairs={{0,7},{1,8},{2,9},{3,10},{4,11},{5,12},{6,13},{7,14},{8,15},{9,0},... | collective-permute-start | bytes 393224 | tf_op jit(solution)/shard_map/ppermute | solution.py:468
  119.4 5.2 %rest.1.refs_16_ = bf16[8,512,512]{2,1,0:T(8,128)(2,1)} custom-call(s32[8]{0:T(128)S(1)} %copy-done.2, s32[72]{0:T(128)S(1)} %broadcast_minimum_fusion.spot, s32[8]{0:T(128)S(1)} %select_reduce_fusion.2.base, bf16[8,512,512]{2,1,0:T(8,128)(2,1)S(1)} %get-tuple-element.66.held, f32[8,512,512]{2,1,0:T(8,128)S(1)} %get-tuple-element.47.inverse, ...), custom_call_target="tpu_custom_call" | custom-call | tf_op jit(solution)/shard_map/rest/pallas_call | solution.py:357
  124.6 6.2 %collective-permute-done.8.refs_7_ = bf16[4,128,128]{2,1,0:T(8,128)(2,1)S(1)} collective-permute-done((bf16[4,128,128]{2,1,0:T(8,128)(2,1)S(1)}, bf16[4,128,128]{2,1,0:T(8,128)(2,1)S(1)}, u32[]{:S(2)}, u32[]{:S(2)}) %collective-permute-start.8) | collective-permute-done | bytes 131104 | tf_op jit(solution)/shard_map/ppermute | solution.py:468
  130.8 2.0 %listed.2 = bf16[8,512,512]{2,1,0:T(8,128)(2,1)} custom-call(s32[32]{0:T(128)S(1)} %copy-done.3, s32[64]{0:T(128)S(1)} %broadcast_add_fusion.1.table, bf16[32,128,128]{2,1,0:T(8,128)(2,1)S(1)} %get-tuple-element.46.pairs, f32[8,512,512]{2,1,0:T(8,128)S(1)} %get-tuple-element.47.inverse, ...), custom_call_target="tpu_custom_call", output_to_operand_aliasing={{}: (20, {})} | custom-call | tf_op jit(solution)/shard_map/listed/pallas_call | solution.py:396
  (49 shorter events, 6.2 us)
Async XLA Ops:
  0.0 9.9 %collective-permute-start = (s32[32]{0:T(128)}, s32[32]{0:T(128)S(1)}, u32[]{:S(2)}, u32[]{:S(2)}) collective-permute-start(s32[32]{0:T(128)} %listed.3), channel_id=1, source_target_pairs={{0,128},{16,144},{32,160},{48,176},{64,192},{80,208},{96,224},{112... | collective-permute-start | bytes 392 | tf_op jit(solution)/shard_map/ppermute | solution.py:424
  10.5 10.5 %copy-start.1 = (f32[8,512]{1,0:T(8,128)S(1)}, f32[8,512]{1,0:T(8,128)}, u32[]{:S(2)}) copy-start(f32[8,512]{1,0:T(8,128)} %energy) | copy-start | bytes 49156
  10.5 10.5 %copy-start.3 = (s32[32]{0:T(128)S(1)}, s32[32]{0:T(128)}, u32[]{:S(2)}) copy-start(s32[32]{0:T(128)} %listed.3) | copy-start | bytes 388
  17.7 8.5 %copy-start.4 = (s32[32]{0:T(128)S(1)}, s32[32]{0:T(128)}, u32[]{:S(2)}) copy-start(s32[32]{0:T(128)} %param.13) | copy-start | bytes 388
  17.7 36.4 %copy-start.2 = (s32[8]{0:T(128)S(1)}, s32[8]{0:T(128)}, u32[]{:S(2)}) copy-start(s32[8]{0:T(128)} %orders.4) | copy-start | bytes 100
  17.7 36.4 %copy-start.5 = (s32[8]{0:T(128)S(1)}, s32[8]{0:T(128)}, u32[]{:S(2)}) copy-start(s32[8]{0:T(128)} %partner.1) | copy-start | bytes 100
  17.7 25.5 %collective-permute-start.1 = (bf16[32,128,128]{2,1,0:T(8,128)(2,1)}, bf16[32,128,128]{2,1,0:T(8,128)(2,1)S(1)}, u32[]{:S(2)}, u32[]{:S(2)}) collective-permute-start(bf16[32,128,128]{2,1,0:T(8,128)(2,1)} %get-tuple-element.45), channel_id=1, source_target_pairs={{0,128},{16,144},{32,160},{48,176},{64,192},{80,208},{96,224},{112... | collective-permute-start | bytes 3145736 | tf_op jit(solution)/shard_map/ppermute | solution.py:424
  17.9 101.3 %collective-permute-start.18 = (bf16[16,448,128]{2,1,0:T(8,128)(2,1)}, bf16[16,448,128]{2,1,0:T(8,128)(2,1)S(1)}, u32[]{:S(2)}, u32[]{:S(2)}) collective-permute-start(bf16[16,448,128]{2,1,0:T(8,128)(2,1)} %get-tuple-element.68), channel_id=1, source_target_pairs={{0,128},{16,144},{32,160},{48,176},{64,192},{80,208},{96,224},{112... | collective-permute-start | bytes 5505032 | tf_op jit(solution)/shard_map/ppermute | solution.py:424
  20.9 89.8 %collective-permute-start.17 = (bf16[40,128,128]{2,1,0:T(8,128)(2,1)}, bf16[40,128,128]{2,1,0:T(8,128)(2,1)S(1)}, u32[]{:S(2)}, u32[]{:S(2)}) collective-permute-start(bf16[40,128,128]{2,1,0:T(8,128)(2,1)} %get-tuple-element.67), channel_id=1, source_target_pairs={{0,128},{16,144},{32,160},{48,176},{64,192},{80,208},{96,224},{112... | collective-permute-start | bytes 3932168 | tf_op jit(solution)/shard_map/ppermute | solution.py:424
  44.5 19.8 %collective-permute-start.10 = (bf16[4,128,128]{2,1,0:T(8,128)(2,1)S(1)}, bf16[4,128,128]{2,1,0:T(8,128)(2,1)S(1)}, u32[]{:S(2)}, u32[]{:S(2)}) collective-permute-start(bf16[4,128,128]{2,1,0:T(8,128)(2,1)S(1)} %get-tuple-element.57), channel_id=1, source_target_pairs={{0,9},{1,10},{2,11},{3,12},{4,13},{5,14},{6,15},{7,0},{8,1},{9,2},... | collective-permute-start | bytes 393224 | tf_op jit(solution)/shard_map/ppermute | solution.py:468
  54.2 19.3 %collective-permute-start.11 = (bf16[4,128,128]{2,1,0:T(8,128)(2,1)S(1)}, bf16[4,128,128]{2,1,0:T(8,128)(2,1)S(1)}, u32[]{:S(2)}, u32[]{:S(2)}) collective-permute-start(bf16[4,128,128]{2,1,0:T(8,128)(2,1)S(1)} %get-tuple-element.58), channel_id=1, source_target_pairs={{0,10},{1,11},{2,12},{3,13},{4,14},{5,15},{6,0},{7,1},{8,2},{9,3},... | collective-permute-start | bytes 393224 | tf_op jit(solution)/shard_map/ppermute | solution.py:468
  54.2 25.4 %collective-permute-start.12 = (bf16[4,128,128]{2,1,0:T(8,128)(2,1)S(1)}, bf16[4,128,128]{2,1,0:T(8,128)(2,1)S(1)}, u32[]{:S(2)}, u32[]{:S(2)}) collective-permute-start(bf16[4,128,128]{2,1,0:T(8,128)(2,1)S(1)} %get-tuple-element.59), channel_id=1, source_target_pairs={{0,11},{1,12},{2,13},{3,14},{4,15},{5,0},{6,1},{7,2},{8,3},{9,4},{... | collective-permute-start | bytes 393224 | tf_op jit(solution)/shard_map/ppermute | solution.py:468
  64.2 19.4 %collective-permute-start.13 = (bf16[4,128,128]{2,1,0:T(8,128)(2,1)S(1)}, bf16[4,128,128]{2,1,0:T(8,128)(2,1)S(1)}, u32[]{:S(2)}, u32[]{:S(2)}) collective-permute-start(bf16[4,128,128]{2,1,0:T(8,128)(2,1)S(1)} %get-tuple-element.60), channel_id=1, source_target_pairs={{0,12},{1,13},{2,14},{3,15},{4,0},{5,1},{6,2},{7,3},{8,4},{9,5},{1... | collective-permute-start | bytes 393224 | tf_op jit(solution)/shard_map/ppermute | solution.py:468
  73.5 12.9 %collective-permute-start.14 = (bf16[4,128,128]{2,1,0:T(8,128)(2,1)S(1)}, bf16[4,128,128]{2,1,0:T(8,128)(2,1)S(1)}, u32[]{:S(2)}, u32[]{:S(2)}) collective-permute-start(bf16[4,128,128]{2,1,0:T(8,128)(2,1)S(1)} %get-tuple-element.61), channel_id=1, source_target_pairs={{0,13},{1,14},{2,15},{3,0},{4,1},{5,2},{6,3},{7,4},{8,5},{9,6},{10... | collective-permute-start | bytes 393224 | tf_op jit(solution)/shard_map/ppermute | solution.py:468
  79.6 9.5 %collective-permute-start.15 = (bf16[4,128,128]{2,1,0:T(8,128)(2,1)S(1)}, bf16[4,128,128]{2,1,0:T(8,128)(2,1)S(1)}, u32[]{:S(2)}, u32[]{:S(2)}) collective-permute-start(bf16[4,128,128]{2,1,0:T(8,128)(2,1)S(1)} %get-tuple-element.62), channel_id=1, source_target_pairs={{0,14},{1,15},{2,0},{3,1},{4,2},{5,3},{6,4},{7,5},{8,6},{9,7},{10,... | collective-permute-start | bytes 393224 | tf_op jit(solution)/shard_map/ppermute | solution.py:468
  83.6 6.3 %collective-permute-start.16 = (bf16[4,128,128]{2,1,0:T(8,128)(2,1)S(1)}, bf16[4,128,128]{2,1,0:T(8,128)(2,1)S(1)}, u32[]{:S(2)}, u32[]{:S(2)}) collective-permute-start(bf16[4,128,128]{2,1,0:T(8,128)(2,1)S(1)} %get-tuple-element.63), channel_id=1, source_target_pairs={{0,15},{1,0},{2,1},{3,2},{4,3},{5,4},{6,5},{7,6},{8,7},{9,8},{10,9... | collective-permute-start | bytes 393224 | tf_op jit(solution)/shard_map/ppermute | solution.py:468
  86.4 4.5 %collective-permute-start.2 = (bf16[4,128,128]{2,1,0:T(8,128)(2,1)S(1)}, bf16[4,128,128]{2,1,0:T(8,128)(2,1)S(1)}, u32[]{:S(2)}, u32[]{:S(2)}) collective-permute-start(bf16[4,128,128]{2,1,0:T(8,128)(2,1)S(1)} %get-tuple-element.49), channel_id=1, source_target_pairs={{0,1},{1,2},{2,3},{3,4},{4,5},{5,6},{6,7},{7,8},{8,9},{9,10},{10,1... | collective-permute-start | bytes 393224 | tf_op jit(solution)/shard_map/ppermute | solution.py:468
  89.2 7.5 %collective-permute-start.3 = (bf16[4,128,128]{2,1,0:T(8,128)(2,1)S(1)}, bf16[4,128,128]{2,1,0:T(8,128)(2,1)S(1)}, u32[]{:S(2)}, u32[]{:S(2)}) collective-permute-start(bf16[4,128,128]{2,1,0:T(8,128)(2,1)S(1)} %get-tuple-element.50), channel_id=1, source_target_pairs={{0,2},{1,3},{2,4},{3,5},{4,6},{5,7},{6,8},{7,9},{8,10},{9,11},{10,... | collective-permute-start | bytes 393224 | tf_op jit(solution)/shard_map/ppermute | solution.py:468
  89.9 8.0 %collective-permute-start.4 = (bf16[4,128,128]{2,1,0:T(8,128)(2,1)S(1)}, bf16[4,128,128]{2,1,0:T(8,128)(2,1)S(1)}, u32[]{:S(2)}, u32[]{:S(2)}) collective-permute-start(bf16[4,128,128]{2,1,0:T(8,128)(2,1)S(1)} %get-tuple-element.51), channel_id=1, source_target_pairs={{0,3},{1,4},{2,5},{3,6},{4,7},{5,8},{6,9},{7,10},{8,11},{9,12},{10... | collective-permute-start | bytes 393224 | tf_op jit(solution)/shard_map/ppermute | solution.py:468
  90.9 33.7 %collective-permute-start.5 = (bf16[4,128,128]{2,1,0:T(8,128)(2,1)S(1)}, bf16[4,128,128]{2,1,0:T(8,128)(2,1)S(1)}, u32[]{:S(2)}, u32[]{:S(2)}) collective-permute-start(bf16[4,128,128]{2,1,0:T(8,128)(2,1)S(1)} %get-tuple-element.52), channel_id=1, source_target_pairs={{0,4},{1,5},{2,6},{3,7},{4,8},{5,9},{6,10},{7,11},{8,12},{9,13},{1... | collective-permute-start | bytes 393224 | tf_op jit(solution)/shard_map/ppermute | solution.py:468
  96.6 28.0 %collective-permute-start.6 = (bf16[4,128,128]{2,1,0:T(8,128)(2,1)S(1)}, bf16[4,128,128]{2,1,0:T(8,128)(2,1)S(1)}, u32[]{:S(2)}, u32[]{:S(2)}) collective-permute-start(bf16[4,128,128]{2,1,0:T(8,128)(2,1)S(1)} %get-tuple-element.53), channel_id=1, source_target_pairs={{0,5},{1,6},{2,7},{3,8},{4,9},{5,10},{6,11},{7,12},{8,13},{9,14},{... | collective-permute-start | bytes 393224 | tf_op jit(solution)/shard_map/ppermute | solution.py:468
  98.0 26.7 %collective-permute-start.7 = (bf16[4,128,128]{2,1,0:T(8,128)(2,1)S(1)}, bf16[4,128,128]{2,1,0:T(8,128)(2,1)S(1)}, u32[]{:S(2)}, u32[]{:S(2)}) collective-permute-start(bf16[4,128,128]{2,1,0:T(8,128)(2,1)S(1)} %get-tuple-element.54), channel_id=1, source_target_pairs={{0,6},{1,7},{2,8},{3,9},{4,10},{5,11},{6,12},{7,13},{8,14},{9,15},... | collective-permute-start | bytes 393224 | tf_op jit(solution)/shard_map/ppermute | solution.py:468
  110.7 20.1 %collective-permute-start.8 = (bf16[4,128,128]{2,1,0:T(8,128)(2,1)S(1)}, bf16[4,128,128]{2,1,0:T(8,128)(2,1)S(1)}, u32[]{:S(2)}, u32[]{:S(2)}) collective-permute-start(bf16[4,128,128]{2,1,0:T(8,128)(2,1)S(1)} %get-tuple-element.55), channel_id=1, source_target_pairs={{0,7},{1,8},{2,9},{3,10},{4,11},{5,12},{6,13},{7,14},{8,15},{9,0},... | collective-permute-start | bytes 393224 | tf_op jit(solution)/shard_map/ppermute | solution.py:468
  119.2 11.6 %collective-permute-start.9 = (bf16[4,128,128]{2,1,0:T(8,128)(2,1)S(1)}, bf16[4,128,128]{2,1,0:T(8,128)(2,1)S(1)}, u32[]{:S(2)}, u32[]{:S(2)}) collective-permute-start(bf16[4,128,128]{2,1,0:T(8,128)(2,1)S(1)} %get-tuple-element.56), channel_id=1, source_target_pairs={{0,8},{1,9},{2,10},{3,11},{4,12},{5,13},{6,14},{7,15},{8,0},{9,1},... | collective-permute-start | bytes 393224 | tf_op jit(solution)/shard_map/ppermute | solution.py:468
  (2 other events, 2.8 us)
